TPU v7x, 32 devices: a whole 2x2x4 slice. The times are simulated.
32 devices in a mesh: atlas: 4 (over y, x), row: 2 (over core), col: 4 (over z).
Axes of the slice: x: 2, y: 2, z: 4, core: 2. Of those that a mesh axis runs over, the one named last changes fastest.
Arguments:
- cells: bfloat16 [4, 64, 1024], P('atlas', None, 'row'), may hold values from -4 to 4
- support: bfloat16 [64, 16384], P(None, 'col'), may hold values from -4 to 4
Outputs:
- cell_dual: float32 [4, 1024], P('atlas', 'row')
- support_dual: float32 [4, 16384], P('atlas', 'col')
- new_support: float32 [64, 16384], P(None, 'col')
All inputs are finite; a program needn't handle non-finite values.
Results may differ from a plain program's by a relative error of at most 0.001.
Values sent between devices are 32-bit elements; how exact they have to be, the bound alone decides.
No kernel may reach another device: no remote copies, remote signals or barrier semaphores. Data moves between devices by JAX's collectives and lax.ppermute only.
A program may use at most 64 MiB of HBM per device.

v0:
```python
import jax
import jax.numpy as jnp
from jax import lax
from jax.sharding import PartitionSpec as P

ITERS = 2
blur = 0.1


def combined_all(value, axis, join):
    pieces = jax.tree.map(lambda part: lax.all_gather(part, axis), value)
    head = jax.tree.map(lambda part: part[0], pieces)
    tail = jax.tree.map(lambda part: part[1:], pieces)
    subtotal, _ = lax.scan(lambda subtotal, slab: (join(subtotal, slab), None), head, tail)
    return subtotal


def lse_pair(first, second):
    top_one, total_one = first
    top_two, total_two = second
    peak = jnp.maximum(top_one, top_two)
    return (peak, total_one * jnp.exp(top_one - peak) + total_two * jnp.exp(top_two - peak))


def shards(cells, support):
    points = cells[0]
    dims, rows = points.shape
    columns = support.shape[1]
    width_block = min(512, columns)
    count = columns // width_block
    points_wide = points.astype(jnp.float32)
    squares_x = jnp.sum(jnp.square(points_wide), axis=0)
    squares_y = jnp.sum(jnp.square(support.astype(jnp.float32)), axis=0)
    total_cells = rows * lax.axis_size("row")
    total_support = columns * lax.axis_size("col")
    atlases = lax.axis_size("atlas")

    def tile_cost(start):
        piece = lax.dynamic_slice_in_dim(support, start, width_block, 1)
        near = lax.dynamic_slice_in_dim(squares_y, start, width_block, 0)
        cross = lax.dot_general(
            points, piece, (((0,), (0,)), ((), ())), preferred_element_type=jnp.float32
        )
        return (squares_x[:, None] + near[None, :] - 2.0 * cross) / dims

    def row_step(dual_g):

        def row_visit(index, carry):
            top, total = carry
            start = index * width_block
            gpart = lax.dynamic_slice_in_dim(dual_g, start, width_block, 0)
            logits = (gpart[None, :] - tile_cost(start)) / blur
            peak = jnp.maximum(top, jnp.max(logits, axis=1))
            total = total * jnp.exp(top - peak) + jnp.sum(jnp.exp(logits - peak[:, None]), axis=1)
            return (peak, total)

        start_carry = (jnp.full((rows,), -jnp.inf, jnp.float32), jnp.zeros((rows,), jnp.float32))
        top, total = lax.fori_loop(0, count, row_visit, start_carry)
        top, total = combined_all((top, total), "col", lse_pair)
        return blur * jnp.log(1.0 / total_cells) - blur * (top + jnp.log(total))

    def column_step(dual_f):

        def column_visit(index, carry):
            top, total = carry
            start = index * width_block
            logits = (dual_f[:, None] - tile_cost(start)) / blur
            peak = jnp.max(logits, axis=0)
            mass = jnp.sum(jnp.exp(logits - peak[None, :]), axis=0)
            return (
                lax.dynamic_update_slice_in_dim(top, peak, start, 0),
                lax.dynamic_update_slice_in_dim(total, mass, start, 0),
            )

        start_carry = (jnp.zeros((columns,), jnp.float32), jnp.zeros((columns,), jnp.float32))
        top, total = lax.fori_loop(0, count, column_visit, start_carry)
        top, total = combined_all((top, total), "row", lse_pair)
        return blur * jnp.log(1.0 / total_support) - blur * (top + jnp.log(total))

    dual_g = jnp.zeros((columns,), jnp.float32)
    dual_f = jnp.zeros((rows,), jnp.float32)
    for step in range(ITERS):
        dual_f = row_step(dual_g)
        dual_g = column_step(dual_f)

    def positions_visit(index, summed):
        start = index * width_block
        gpart = lax.dynamic_slice_in_dim(dual_g, start, width_block, 0)
        plan = jnp.exp((dual_f[:, None] + gpart[None, :] - tile_cost(start)) / blur)
        moved = jnp.dot(points_wide, plan, precision=lax.Precision.HIGHEST) * total_support
        return lax.dynamic_update_slice_in_dim(summed, moved, start, 1)

    terms = lax.fori_loop(0, count, positions_visit, jnp.zeros((dims, columns), jnp.float32))
    summed = lax.psum(terms, ("atlas", "row"))
    updated = summed / atlases
    return (dual_f[None, :], dual_g[None, :], updated)


def solution(mesh):
    in_specs = (P("atlas", None, "row"), P(None, "col"))
    out_specs = (P("atlas", "row"), P("atlas", "col"), P(None, "col"))
    return jax.shard_map(shards, mesh=mesh, in_specs=in_specs, out_specs=out_specs, check_vma=False)
```

profile of v0, /device:TPU:0, one launch (start us, length us, event | category | flops | bytes accessed | tf_op | source)
XLA Modules:
  0.0 182.5 jit_solution(9270883459431666822)
XLA Ops:
  7.3 0.9 multiply_reduce_fusion.1
  8.2 1.2 multiply_reduce_fusion
  9.4 6.2 %while.114 = (s32[]{:T(128)}, f32[512]{0:T(512)S(1)}, f32[512]{0:T(512)S(1)}, f32[512]{0:T(512)S(1)}, f32[4096]{0:T(1024)S(1)}, /*index=5*/bf16[64,4096]{1,0:T(8...) while((s32[]{:T(128)}, f32[512]{0:T(512)S(1)}, ...), condition=%wide.region_5.0_spmd.clone, body=%wide.region_2.0_spmd.clone.sunk | while | flops 35916292 | bytes 2263222 | solution.py:58
  15.6 13.6 %all-gather.8 = f32[4,1,512]{2,1,0:T(1,128)S(1)} all-gather(f32[1,1,512]{2,1,0:T(1,128)S(1)} %bitcast.124), channel_id=2, replica_groups=mesh['atlas'=4,'row'=2,'col'=4] {'col'}, dimensions={0}, use_global_device_ids=true | all-gather | bytes 10240 | tf_op jit(solution)/shard_map/all_gather | solution.py:11
  29.9 11.9 %all-gather.9 = f32[4,1,512]{2,1,0:T(1,128)S(1)} all-gather(f32[1,1,512]{2,1,0:T(1,128)S(1)} %bitcast.134), channel_id=3, replica_groups=mesh['atlas'=4,'row'=2,'col'=4] {'col'}, dimensions={0}, use_global_device_ids=true | all-gather | bytes 10240 | tf_op jit(solution)/shard_map/all_gather | solution.py:11
  41.8 0.7 slice-done.3
  42.5 0.7 slice-done.2
  43.4 10.0 %while.110 = (s32[]{:T(128)}, f32[4096]{0:T(1024)S(1)}, f32[4096]{0:T(1024)S(1)}, f32[512]{0:T(512)S(1)}, f32[512]{0:T(512)S(1)}, /*index=5*/f32[4096]{0:T(1024)...) while((s32[]{:T(128)}, f32[4096]{0:T(1024)S(1)}, ...), condition=%wide.region_11.12_spmd, body=%wide.region_8.11_spmd.sunk | while | flops 35912708 | bytes 2252979 | solution.py:76
  53.4 1.8 all-gather.3
  55.2 1.8 all-gather.2
  57.0 6.8 %while.115 = (s32[]{:T(128)}, f32[512]{0:T(512)S(1)}, f32[512]{0:T(512)S(1)}, f32[4096]{0:T(1024)S(1)}, f32[512]{0:T(512)S(1)}, /*index=5*/f32[4096]{0:T(1024)S(...) while((s32[]{:T(128)}, f32[512]{0:T(512)S(1)}, ...), condition=%wide.region_15.16_spmd.clone, body=%wide.region_12.0_spmd.clone.sunk | while | flops 35916292 | bytes 2269378 | solution.py:58
  63.9 11.9 %all-gather.10 = f32[4,1,512]{2,1,0:T(1,128)S(1)} all-gather(f32[1,1,512]{2,1,0:T(1,128)S(1)} %bitcast.123), channel_id=6, replica_groups=mesh['atlas'=4,'row'=2,'col'=4] {'col'}, dimensions={0}, use_global_device_ids=true | all-gather | bytes 10240 | tf_op jit(solution)/shard_map/all_gather | solution.py:11
  76.4 11.9 %all-gather.11 = f32[4,1,512]{2,1,0:T(1,128)S(1)} all-gather(f32[1,1,512]{2,1,0:T(1,128)S(1)} %bitcast.133), channel_id=7, replica_groups=mesh['atlas'=4,'row'=2,'col'=4] {'col'}, dimensions={0}, use_global_device_ids=true | all-gather | bytes 10240 | tf_op jit(solution)/shard_map/all_gather | solution.py:11
  88.3 0.6 copy-done.5
  88.9 0.7 slice-done.1
  89.6 0.7 slice-done.5
  90.3 0.7 slice-done.4
  91.2 10.0 %while.112 = (s32[]{:T(128)}, f32[4096]{0:T(1024)S(1)}, f32[4096]{0:T(1024)S(1)}, f32[512]{0:T(512)S(1)}, f32[512]{0:T(512)S(1)}, /*index=5*/f32[4096]{0:T(1024)...) while((s32[]{:T(128)}, f32[4096]{0:T(1024)S(1)}, ...), condition=%wide.region_21.22_spmd, body=%wide.region_18.0_spmd.sunk | while | flops 35912708 | bytes 2252979 | solution.py:76
  101.2 1.8 all-gather.7
  103.0 1.8 all-gather.6
  104.9 12.0 %while.113 = (s32[]{:T(128)}, f32[64,4096]{1,0:T(8,128)S(1)}, f32[512]{0:T(512)S(1)}, f32[4096]{0:T(1024)S(1)}, f32[512]{0:T(512)S(1)}, /*index=5*/f32[4096]{0:T...) while((s32[]{:T(128)}, f32[64,4096]{1,0:T(8,128)S(1)}, ...), condition=%wide.region_23.24_spmd, body=%wide.region_22.23_spmd.sunk | while | flops 236748800 | bytes 2506939 | solution.py:93
  105.6 0.8 fusion.86
  107.1 0.8 fusion.86
  108.6 0.8 fusion.86
  110.1 0.8 fusion.86
  111.6 0.8 fusion.86
  113.1 0.8 fusion.86
  114.6 0.8 fusion.86
  116.1 0.8 fusion.86
  117.9 0.7 multiply_subtract_fusion.1
  118.6 54.8 %all-reduce.2.cloned.1.call-done = f32[64,4096]{1,0:T(8,128)} async-done(((f32[64,4096]{1,0:T(8,128)}), f32[64,4096]{1,0:T(8,128)}) %all-reduce.2.cloned.1.call-update) | async-done | bytes 1048592 | tf_op jit(solution)/shard_map/psum | solution.py:94
  173.4 2.3 %broadcast_multiply_fusion = f32[64,4096]{1,0:T(8,128)} fusion(f32[64,4096]{1,0:T(8,128)} %all-reduce.2.cloned.1.call-done), kind=kLoop, calls=%fused_computation.61 | loop fusion | flops 262144 | bytes 2097152 | tf_op jit(solution)/shard_map/div | solution.py:95
  (264 shorter events, 40.7 us)
Async XLA Ops:
  7.2 2.2 %copy-start.1 = (bf16[64,4096]{1,0:T(8,128)(2,1)S(1)}, bf16[64,4096]{1,0:T(8,128)(2,1)}, u32[]{:S(2)}) copy-start(bf16[64,4096]{1,0:T(8,128)(2,1)} %param.17) | copy-start | bytes 1572868
  7.2 166.2 %all-reduce.2.cloned.1.call-start = ((), (), s32[]{:S(2)}) async-start(), calls=%async_computation | async-start | bytes 2097152 | tf_op jit(solution)/shard_map/psum | solution.py:94
  8.2 1.2 copy-start.2
  29.3 0.6 copy-start.4
  41.8 0.7 slice-start.3
  42.5 0.7 slice-start.2
  75.8 0.6 copy-start.3
  88.3 0.6 copy-start.5
  88.9 0.7 slice-start.1
  89.6 0.7 slice-start.5
  90.3 0.7 slice-start.4
  90.3 0.7 slice-start
  116.9 0.6 copy-start.6
  116.9 1.0 copy-start
Sparse Core Ops, SparseCore 0:
  118.0 55.2 all-reduce.1
where the time goes:
time: 183 us; the launch traced here: 182 us
  blocking collectives  56.7 us (31%)
  waiting for transfers between devices  54.8 us (30%)
  matrix products  25.1 us (14%)
  local copies, waits for them, and re-layouts  18.8 us (10%)
  between operations  14.2 us (8%)
  other arithmetic  12 us (7%)
    all_gather x8, blocking collectives, combined_all(): pieces = jax.tree.map(lambda part: lax.all_gather(part, axis), value)  56.7 us
    psum x1, waiting for transfers between devices, shards(): summed = lax.psum(terms, ('atlas', 'row'))  54.8 us
    dot_general x40, matrix products, tile_cost(): lax.dot_general(points, piece, (((0,), (0,)), ((), ())), preferred_elemen...  18.7 us
    dot_general x8, matrix products, positions_visit(): jnp.dot(points_wide, plan, precision=lax.Precision.HIGHEST) * total_support  6.37 us
    dynamic_update_slice x16, local copies, waits for them, and re-layouts, column_visit(): lax.dynamic_update_slice_in_dim(top, peak, start, 0)  4.3 us
    dynamic_update_slice x16, local copies, waits for them, and re-layouts, column_visit(): lax.dynamic_update_slice_in_dim(total, mass, start, 0)  3.85 us
  transfers between devices with their start and end apart: 1, of which 1 were waited for; matrix products, arithmetic and copies ran while one was open for 0% of the time, Pallas kernels for 0%

commit v1 on v0

--- a/solution.py
+++ b/solution.py
@@ -91,7 +91,8 @@
         return lax.dynamic_update_slice_in_dim(summed, moved, start, 1)
 
     terms = lax.fori_loop(0, count, positions_visit, jnp.zeros((dims, columns), jnp.float32))
-    summed = lax.psum(terms, ("atlas", "row"))
+    half = lax.psum(terms, "atlas")
+    summed = lax.psum(half, "row")
     updated = summed / atlases
     return (dual_f[None, :], dual_g[None, :], updated)
 

time: 183 us -> 200 us (1.093)
  waiting for transfers between devices: 54.8 us -> 72.3 us
    psum x1 -> x2, waiting for transfers between devices: 54.8 us -> 72.2 us  [the longest x1 51.1 us: shards(): half = lax.psum(terms, 'atlas')]
  transfers between devices with their start and end apart: 1 -> 2, of which waited for: 1 -> 2; matrix products, arithmetic and copies ran while one was open for 0% -> 0% of each run, Pallas kernels for 0% -> 0%
where the time goes in v1:
time: 200 us
  waiting for transfers between devices  72.3 us (36%)
  blocking collectives  56.7 us (28%)
  matrix products  25.1 us (13%)
  local copies, waits for them, and re-layouts  18.8 us (9%)
  between operations  14.2 us (7%)
  other arithmetic  12 us (6%)
    all_gather x8, blocking collectives, combined_all(): pieces = jax.tree.map(lambda part: lax.all_gather(part, axis), value)  56.7 us
    psum x1, waiting for transfers between devices, shards(): half = lax.psum(terms, 'atlas')  51.1 us
    psum x1, waiting for transfers between devices, shards(): summed = lax.psum(half, 'row')  21.1 us
    dot_general x40, matrix products, tile_cost(): lax.dot_general(points, piece, (((0,), (0,)), ((), ())), preferred_elemen...  18.7 us
    dot_general x8, matrix products, positions_visit(): jnp.dot(points_wide, plan, precision=lax.Precision.HIGHEST) * total_support  6.37 us
    dynamic_update_slice x16, local copies, waits for them, and re-layouts, column_visit(): lax.dynamic_update_slice_in_dim(top, peak, start, 0)  4.3 us
  transfers between devices with their start and end apart: 2, of which 2 were waited for; matrix products, arithmetic and copies ran while one was open for 0% of the time, Pallas kernels for 0%

profile of v1, /device:TPU:0, one launch (start us, length us, event | category | flops | bytes accessed | tf_op | source)
XLA Modules:
  0.0 200.0 jit_solution(7314482372878963799)
XLA Ops:
  7.3 0.9 multiply_reduce_fusion.1
  8.2 1.2 multiply_reduce_fusion
  9.4 6.2 %while.114 = (s32[]{:T(128)}, f32[512]{0:T(512)S(1)}, f32[512]{0:T(512)S(1)}, f32[512]{0:T(512)S(1)}, f32[4096]{0:T(1024)S(1)}, /*index=5*/bf16[64,4096]{1,0:T(8...) while((s32[]{:T(128)}, f32[512]{0:T(512)S(1)}, ...), condition=%wide.region_5.0_spmd.clone, body=%wide.region_2.0_spmd.clone.sunk | while | flops 35916292 | bytes 2263222 | solution.py:58
  15.6 13.6 %all-gather.8 = f32[4,1,512]{2,1,0:T(1,128)S(1)} all-gather(f32[1,1,512]{2,1,0:T(1,128)S(1)} %bitcast.124), channel_id=2, replica_groups=mesh['atlas'=4,'row'=2,'col'=4] {'col'}, dimensions={0}, use_global_device_ids=true | all-gather | bytes 10240 | tf_op jit(solution)/shard_map/all_gather | solution.py:11
  29.9 11.9 %all-gather.9 = f32[4,1,512]{2,1,0:T(1,128)S(1)} all-gather(f32[1,1,512]{2,1,0:T(1,128)S(1)} %bitcast.134), channel_id=3, replica_groups=mesh['atlas'=4,'row'=2,'col'=4] {'col'}, dimensions={0}, use_global_device_ids=true | all-gather | bytes 10240 | tf_op jit(solution)/shard_map/all_gather | solution.py:11
  41.8 0.7 slice-done.3
  42.5 0.7 slice-done.2
  43.4 10.0 %while.110 = (s32[]{:T(128)}, f32[4096]{0:T(1024)S(1)}, f32[4096]{0:T(1024)S(1)}, f32[512]{0:T(512)S(1)}, f32[512]{0:T(512)S(1)}, /*index=5*/f32[4096]{0:T(1024)...) while((s32[]{:T(128)}, f32[4096]{0:T(1024)S(1)}, ...), condition=%wide.region_11.12_spmd, body=%wide.region_8.11_spmd.sunk | while | flops 35912708 | bytes 2252979 | solution.py:76
  53.4 1.8 all-gather.3
  55.2 1.8 all-gather.2
  57.0 6.8 %while.115 = (s32[]{:T(128)}, f32[512]{0:T(512)S(1)}, f32[512]{0:T(512)S(1)}, f32[4096]{0:T(1024)S(1)}, f32[512]{0:T(512)S(1)}, /*index=5*/f32[4096]{0:T(1024)S(...) while((s32[]{:T(128)}, f32[512]{0:T(512)S(1)}, ...), condition=%wide.region_15.16_spmd.clone, body=%wide.region_12.0_spmd.clone.sunk | while | flops 35916292 | bytes 2269378 | solution.py:58
  63.9 11.9 %all-gather.10 = f32[4,1,512]{2,1,0:T(1,128)S(1)} all-gather(f32[1,1,512]{2,1,0:T(1,128)S(1)} %bitcast.123), channel_id=6, replica_groups=mesh['atlas'=4,'row'=2,'col'=4] {'col'}, dimensions={0}, use_global_device_ids=true | all-gather | bytes 10240 | tf_op jit(solution)/shard_map/all_gather | solution.py:11
  76.4 11.9 %all-gather.11 = f32[4,1,512]{2,1,0:T(1,128)S(1)} all-gather(f32[1,1,512]{2,1,0:T(1,128)S(1)} %bitcast.133), channel_id=7, replica_groups=mesh['atlas'=4,'row'=2,'col'=4] {'col'}, dimensions={0}, use_global_device_ids=true | all-gather | bytes 10240 | tf_op jit(solution)/shard_map/all_gather | solution.py:11
  88.9 0.7 slice-done.1
  89.6 0.7 slice-done.5
  90.3 0.7 slice-done.4
  91.2 10.0 %while.112 = (s32[]{:T(128)}, f32[4096]{0:T(1024)S(1)}, f32[4096]{0:T(1024)S(1)}, f32[512]{0:T(512)S(1)}, f32[512]{0:T(512)S(1)}, /*index=5*/f32[4096]{0:T(1024)...) while((s32[]{:T(128)}, f32[4096]{0:T(1024)S(1)}, ...), condition=%wide.region_21.22_spmd, body=%wide.region_18.0_spmd.sunk | while | flops 35912708 | bytes 2252979 | solution.py:76
  101.2 1.8 all-gather.7
  103.0 1.8 all-gather.6
  104.9 12.0 %while.113 = (s32[]{:T(128)}, f32[64,4096]{1,0:T(8,128)S(1)}, f32[512]{0:T(512)S(1)}, f32[4096]{0:T(1024)S(1)}, f32[512]{0:T(512)S(1)}, /*index=5*/f32[4096]{0:T...) while((s32[]{:T(128)}, f32[64,4096]{1,0:T(8,128)S(1)}, ...), condition=%wide.region_23.24_spmd, body=%wide.region_22.23_spmd.sunk | while | flops 236748800 | bytes 2506939 | solution.py:93
  105.6 0.8 fusion.86
  107.1 0.8 fusion.86
  108.6 0.8 fusion.86
  110.1 0.8 fusion.86
  111.6 0.8 fusion.86
  113.1 0.8 fusion.86
  114.6 0.8 fusion.86
  116.1 0.8 fusion.86
  118.0 51.1 %all-reduce.3.cloned.1.call-done = f32[64,4096]{1,0:T(8,128)} async-done(((f32[64,4096]{1,0:T(8,128)}), f32[64,4096]{1,0:T(8,128)}) %all-reduce.3.cloned.1.call-update) | async-done | bytes 1048592 | tf_op jit(solution)/shard_map/psum | solution.py:94
  169.1 0.7 multiply_subtract_fusion.1
  169.8 21.1 %all-reduce.5.cloned.1.call-done = f32[64,4096]{1,0:T(8,128)} async-done(((f32[64,4096]{1,0:T(8,128)}), f32[64,4096]{1,0:T(8,128)}) %all-reduce.5.cloned.1.call-update) | async-done | bytes 1048592 | tf_op jit(solution)/shard_map/psum | solution.py:95
  190.9 2.3 %broadcast_multiply_fusion = f32[64,4096]{1,0:T(8,128)} fusion(f32[64,4096]{1,0:T(8,128)} %all-reduce.5.cloned.1.call-done), kind=kLoop, calls=%fused_computation.61 | loop fusion | flops 262144 | bytes 2097152 | tf_op jit(solution)/shard_map/div | solution.py:96
  (267 shorter events, 41.3 us)
Async XLA Ops:
  7.2 2.2 %copy-start.1 = (bf16[64,4096]{1,0:T(8,128)(2,1)S(1)}, bf16[64,4096]{1,0:T(8,128)(2,1)}, u32[]{:S(2)}) copy-start(bf16[64,4096]{1,0:T(8,128)(2,1)} %param.17) | copy-start | bytes 1572868
  7.2 161.9 %all-reduce.3.cloned.1.call-start = ((), (), s32[]{:S(2)}) async-start(), calls=%async_computation | async-start | bytes 2097152 | tf_op jit(solution)/shard_map/psum | solution.py:94
  8.2 1.2 copy-start.2
  29.3 0.6 copy-start.4
  41.8 0.7 slice-start.3
  42.5 0.7 slice-start.2
  75.8 0.6 copy-start.3
  88.3 0.6 copy-start.5
  88.9 0.7 slice-start.1
  89.6 0.7 slice-start.5
  90.3 0.7 slice-start.4
  90.3 0.7 slice-start
  116.9 0.6 copy-start.6
  116.9 1.0 copy-start
  117.9 73.0 %all-reduce.5.cloned.1.call-start = ((), (), s32[]{:S(2)}) async-start(), calls=%async_computation.1 | async-start | bytes 2097152 | tf_op jit(solution)/shard_map/psum | solution.py:95
Sparse Core Ops, SparseCore 0:
  118.0 51.0 all-reduce.2
  171.4 19.4 all-reduce.4
